TPU v7x, 512 devices: a whole 4x8x8 slice. The times are simulated.
512 devices in a mesh: feat: 128 (over x, y, z_hi), rows: 4 (over z_lo, core).
Axes of the slice: x: 4, y: 8, z: 8 (z_hi: 4, z_lo: 2; z = z_hi * 2 + z_lo), core: 2. Of those that a mesh axis runs over, the one named last changes fastest.
Arguments:
- binned: int32 [8192, 8192], P('rows', 'feat'), may hold values from 0 to 255
- node_of: int32 [8192], P('rows'), may hold values from 0 to 31
- margin: float32 [8192], P('rows'), may hold values from -6 to 6
- labels: float32 [8192], P('rows'), may hold values from 0 to 1
- split_feature: int32 [32], replicated, may hold values from 0 to 8191
- split_bin: int32 [32], replicated, may hold values from 0 to 255
Outputs:
- histogram: float32 [32, 2, 8192, 256], P('rows', None, 'feat')
- margin_out: float32 [8192], P('rows')
- child_out: int32 [8192], P('rows')
- grad_out: float32 [2, 8192], P(None, 'rows')
All inputs are finite; a program needn't handle non-finite values.
Results may differ from a plain program's by a relative error of at most 0.0045.
Values may be sent and summed in bfloat16 or wider, within the bound.
No kernel may reach another device: no remote copies, remote signals or barrier semaphores. Data moves between devices by JAX's collectives and lax.ppermute only.
A program may use at most 64 MiB of HBM per device.

v0:
```python
import jax
import jax.numpy as jnp
from jax import lax
from jax.sharding import PartitionSpec as P

BINS = 256


def leaf_table(selected, split_rows):
    below = (jnp.arange(selected.shape[2])[None, :] <= split_rows[:, None]).astype(jnp.float32)
    left = jnp.sum(selected * below[:, None, :], axis=2)
    whole = jnp.sum(selected, axis=2)
    return jnp.concatenate([left, whole], axis=1)


def node_sums(nodes_here, feature_ids, split_rows, feat_start):
    feat_count = nodes_here.shape[2]
    local = feature_ids - feat_start
    owned = (local >= 0) & (local < feat_count)
    chooser = ((local[:, None] == jnp.arange(feat_count)[None, :]) & owned[:, None]).astype(
        jnp.float32
    )
    selected = jnp.einsum("ncfb,nf->ncb", nodes_here, chooser, precision=lax.Precision.HIGHEST)
    return leaf_table(selected, split_rows)


def on_device(binned, node_of, margin, labels, split_feature, split_bin):
    row_count, feat_count = binned.shape
    node_total = split_feature.shape[0]
    feat_start = lax.axis_index("feat") * feat_count
    probability = jax.nn.sigmoid(margin)
    gradient = (probability - labels).astype(jnp.bfloat16)
    hessian = (probability * (1.0 - probability)).astype(jnp.bfloat16)
    node_hot = node_of[:, None] == jnp.arange(node_total, dtype=jnp.int32)[None, :]
    hot_float = node_hot.astype(jnp.bfloat16)
    weights = jnp.stack([gradient[:, None] * hot_float, hessian[:, None] * hot_float], axis=2)
    weights = weights.reshape(row_count, 2 * node_total)
    row_feature = jnp.sum(jnp.where(node_hot, split_feature[None, :], 0), axis=1)
    row_cut = jnp.sum(jnp.where(node_hot, split_bin[None, :], 0), axis=1)
    local = row_feature - feat_start
    owned = (local >= 0) & (local < feat_count)
    column_hot = jnp.arange(feat_count, dtype=jnp.int32)[None, :] == local[:, None]
    row_value = jnp.sum(jnp.where(column_hot, binned, 0), axis=1)
    right_bits = ((row_value > row_cut) & owned).astype(jnp.int32)
    go_right = lax.psum(right_bits, "feat")
    bin_ids = jnp.arange(BINS, dtype=jnp.int32)
    group = 8

    def add_block(block_index, partial_value):
        columns = lax.dynamic_slice_in_dim(binned, block_index * group, group, 1)
        one_hot = (columns.T[:, :, None] == bin_ids[None, None, :]).astype(jnp.bfloat16)
        piece = jnp.einsum("rk,frb->kfb", weights, one_hot, preferred_element_type=jnp.float32)
        return lax.dynamic_update_slice_in_dim(partial_value, piece, block_index * group, 1)

    partial_value = lax.fori_loop(
        0,
        feat_count // group,
        add_block,
        jnp.zeros((2 * node_total, feat_count, BINS), jnp.float32),
    )
    partial_value = partial_value.reshape(node_total, 2, feat_count, BINS).astype(jnp.bfloat16)
    node_share = node_total // lax.axis_size("rows")
    node_start = lax.axis_index("rows") * node_share
    summed = lax.psum(partial_value, "rows").astype(jnp.float32)
    histogram = lax.dynamic_slice_in_dim(summed, node_start, node_share, 0)
    table_part = node_sums(summed, split_feature, split_bin, feat_start)
    table = lax.psum(table_part, "feat")
    leaf_left = -table[:, 0] / (table[:, 1] + 1.0)
    leaf_right = -(table[:, 2] - table[:, 0]) / (table[:, 3] - table[:, 1] + 1.0)
    row_left = jnp.sum(jnp.where(node_hot, leaf_left[None, :], 0.0), axis=1)
    row_right = jnp.sum(jnp.where(node_hot, leaf_right[None, :], 0.0), axis=1)
    margin_out = margin + jnp.where(go_right == 1, row_right, row_left)
    child_out = 2 * node_of + go_right
    fresh = jax.nn.sigmoid(margin_out)
    grad_out = jnp.stack([fresh - labels, fresh * (1.0 - fresh)], axis=0)
    return (histogram, margin_out, child_out, grad_out)


def solution(mesh):
    in_specs = (P("rows", "feat"), P("rows"), P("rows"), P("rows"), P(), P())
    out_specs = (P("rows", None, "feat", None), P("rows"), P("rows"), P(None, "rows"))
    return jax.shard_map(
        on_device, mesh=mesh, in_specs=in_specs, out_specs=out_specs, check_vma=False
    )
```

profile of v0, /device:TPU:64, one launch (start us, length us, event | category | flops | bytes accessed | tf_op | source)
XLA Modules:
  0.0 510.7 jit_solution(691972997853340159)
XLA Ops:
  7.2 0.0 copy-start
  7.2 0.0 all-reduce.2.cloned.1.call-start
  7.2 0.8 subtract_convert_fusion
  8.0 1.1 compare_select_fusion.1
  9.1 0.6 pad_maximum_fusion
  9.7 0.1 reshape.186
  9.8 0.2 broadcast_in_dim.65
  10.1 0.0 copy-done
  10.1 35.7 %while.14 = (s32[]{:T(128)}, bf16[64,64,256]{2,0,1:T(8,128)(2,1)S(1)}, s32[2048,64]{0,1:T(8,128)S(1)}, bf16[2048,64]{0,1:T(8,128)(2,1)S(1)}, s32[]{:T(128)}, /*index=5*/s32[]{:T(128)}, s32[]{:T(128)}, s32[]{:T(128)}) while((s32[]{:T(128)}, bf16[64,64,256]{2,0,1:T(8,128)(2,1)S(1)}, s32[2048,64]{0,1:T(8,128)S(1)}, ...), condition=%wide.region_1.2_spmd.clone, body=%wide.region_0.1_spmd.clone.sunk | while | flops 541065216 | bytes 983187 | solution.py:55
  10.1 4.4 fusion.21
  14.6 4.4 fusion.21
  19.1 4.4 fusion.21
  23.5 4.4 fusion.21
  28.0 4.4 fusion.21
  32.5 4.4 fusion.21
  36.9 4.4 fusion.21
  41.4 4.4 fusion.21
  45.8 2.5 copy.11
  48.3 0.0 copy-start.1
  48.3 0.0 copy-start.5
  48.3 0.0 copy-start.6
  48.3 0.0 copy-start.2
  48.3 0.0 copy-start.3
  48.3 0.0 all-reduce.2.cloned.1.call-update
  48.3 0.6 copy-done.1
  49.0 0.0 copy-done.5
  49.0 0.0 copy-done.6
  49.0 0.2 select_reduce_fusion.3
  49.2 0.1 select_reduce_fusion
  49.3 34.9 %psum.22 = s32[2048]{0:T(1024)S(1)} all-reduce(s32[2048]{0:T(1024)S(1)} %and_convert_fusion), channel_id=1, replica_groups=mesh['feat'=128,'rows'=4] {'feat'}, use_global_device_ids=true, to_apply=%region_6.7 | all-reduce | flops 2048 | bytes 16384 | tf_op jit(solution)/shard_map/psum | solution.py:45
  84.1 0.1 fusion.12
  84.2 0.6 multiply_add_fusion
  84.8 0.1 fusion.10
  84.9 33.3 %all-reduce.2.cloned.1.call-done = bf16[32,2,64,256]{3,2,1,0:T(8,128)(2,1)} async-done(((bf16[32,2,64,256]{3,2,1,0:T(8,128)(2,1)}), bf16[32,2,64,256]{3,2,1,0:T(8,128)(2,1)}) %all-reduce.2.cloned.1.call-update) | async-done | bytes 2097168 | tf_op jit(solution)/shard_map/psum | solution.py:64
  118.2 2.0 fusion.8
  120.2 0.1 fusion.7
  120.3 380.5 %psum.23 = f32[32,4]{0,1:T(4,128)S(1)} all-reduce(f32[32,4]{0,1:T(4,128)S(1)} %pad_maximum_fusion.2), channel_id=1, replica_groups=mesh['feat'=128,'rows'=4] {'feat'}, use_global_device_ids=true, to_apply=%region_9.10 | all-reduce | flops 128 | bytes 1024 | tf_op jit(solution)/shard_map/psum | solution.py:67
  500.8 0.2 select_reduce_fusion.1
  501.0 0.0 copy-done.2
  501.0 0.0 copy-done.3
  501.0 0.0 copy-start.4
  501.1 0.6 pad_maximum_fusion.1
  501.7 2.1 dynamic-slice_convert_fusion
  503.8 0.0 copy-done.4
  (15 shorter events, 0.2 us)
Async XLA Ops:
  7.2 2.9 copy-start
  7.2 111.0 %all-reduce.2.cloned.1.call-start = ((), (), s32[]{:S(2)}) async-start(), calls=%async_computation | async-start | bytes 4194304 | tf_op jit(solution)/shard_map/psum | solution.py:64
  48.3 0.7 copy-start.1
  48.3 0.7 copy-start.5
  48.3 0.7 copy-start.6
  48.3 452.7 %copy-start.2 = (f32[2048]{0:T(1024)S(1)}, f32[2048]{0:T(1024)}, u32[]{:S(2)}) copy-start(f32[2048]{0:T(1024)} %param.11) | copy-start | bytes 24580
  48.3 452.7 %copy-start.3 = (f32[2048]{0:T(1024)S(1)}, f32[2048]{0:T(1024)}, u32[]{:S(2)}) copy-start(f32[2048]{0:T(1024)} %param.10) | copy-start | bytes 24580
  501.0 2.8 copy-start.4
Sparse Core Ops, SparseCore 0:
  48.5 69.6 all-reduce.1
where the time goes:
time: 511 us
  blocking collectives  415 us (81%)
  matrix products  37.3 us (7%)
  waiting for transfers between devices  33.3 us (7%)
  between operations  14.2 us (3%)
  other arithmetic  6.54 us (1%)
    psum x1, blocking collectives, on_device(): table = lax.psum(table_part, 'feat')  381 us
    dot_general x8, matrix products, add_block(): jnp.einsum('rk,frb->kfb', weights, one_hot, preferred_element_type=jnp.fl...  35.3 us
    psum x1, blocking collectives, on_device(): go_right = lax.psum(right_bits, 'feat')  34.9 us
    psum x1, waiting for transfers between devices, on_device(): summed = lax.psum(partial_value, 'rows').astype(jnp.float32)  33.3 us
  transfers between devices with their start and end apart: 1, of which 1 were waited for; matrix products, arithmetic and copies ran while one was open for 0% of the time, Pallas kernels for 0%

commit v1 on v0

--- a/solution.py
+++ b/solution.py
@@ -64,7 +64,7 @@
     summed = lax.psum(partial_value, "rows").astype(jnp.float32)
     histogram = lax.dynamic_slice_in_dim(summed, node_start, node_share, 0)
     table_part = node_sums(summed, split_feature, split_bin, feat_start)
-    table = lax.psum(table_part, "feat")
+    table = jnp.sum(lax.all_gather(table_part, "feat"), axis=0)
     leaf_left = -table[:, 0] / (table[:, 1] + 1.0)
     leaf_right = -(table[:, 2] - table[:, 0]) / (table[:, 3] - table[:, 1] + 1.0)
     row_left = jnp.sum(jnp.where(node_hot, leaf_left[None, :], 0.0), axis=1)

time: 511 us -> 508 us (level)
    psum x1 -> x0, blocking collectives: 381 us -> none  [on_device(): table = lax.psum(table_part, 'feat')]
    all_gather x0 -> x1, blocking collectives: none -> 377 us  [on_device(): table = jnp.sum(lax.all_gather(table_part, 'feat'), axis=0)]
where the time goes in v1:
time: 508 us
  blocking collectives  412 us (81%)
  matrix products  37.3 us (7%)
  waiting for transfers between devices  33.3 us (7%)
  between operations  14.2 us (3%)
  other arithmetic  6.68 us (1%)
    all_gather x1, blocking collectives, on_device(): table = jnp.sum(lax.all_gather(table_part, 'feat'), axis=0)  377 us
    dot_general x8, matrix products, add_block(): jnp.einsum('rk,frb->kfb', weights, one_hot, preferred_element_type=jnp.fl...  35.3 us
    psum x1, blocking collectives, on_device(): go_right = lax.psum(right_bits, 'feat')  34.9 us
    psum x1, waiting for transfers between devices, on_device(): summed = lax.psum(partial_value, 'rows').astype(jnp.float32)  33.3 us
  transfers between devices with their start and end apart: 1, of which 1 were waited for; matrix products, arithmetic and copies ran while one was open for 0% of the time, Pallas kernels for 0%

profile of v1, /device:TPU:64, one launch (start us, length us, event | category | flops | bytes accessed | tf_op | source)
XLA Modules:
  0.0 507.7 jit_solution(5778854965331645247)
XLA Ops:
  7.2 0.0 copy-start
  7.2 0.0 all-reduce.2.cloned.1.call-start
  7.2 0.8 subtract_convert_fusion
  8.0 1.1 compare_select_fusion.1
  9.1 0.6 pad_maximum_fusion
  9.7 0.1 reshape.186
  9.8 0.2 broadcast_in_dim.65
  10.1 0.0 copy-done
  10.1 35.7 %while.14 = (s32[]{:T(128)}, bf16[64,64,256]{2,0,1:T(8,128)(2,1)S(1)}, s32[2048,64]{0,1:T(8,128)S(1)}, bf16[2048,64]{0,1:T(8,128)(2,1)S(1)}, s32[]{:T(128)}, /*index=5*/s32[]{:T(128)}, s32[]{:T(128)}, s32[]{:T(128)}) while((s32[]{:T(128)}, bf16[64,64,256]{2,0,1:T(8,128)(2,1)S(1)}, s32[2048,64]{0,1:T(8,128)S(1)}, ...), condition=%wide.region_1.2_spmd.clone, body=%wide.region_0.1_spmd.clone.sunk | while | flops 541065216 | bytes 983187 | solution.py:55
  10.1 4.4 fusion.21
  14.6 4.4 fusion.21
  19.1 4.4 fusion.21
  23.5 4.4 fusion.21
  28.0 4.4 fusion.21
  32.5 4.4 fusion.21
  36.9 4.4 fusion.21
  41.4 4.4 fusion.21
  45.8 2.5 copy.12
  48.3 0.0 copy-start.1
  48.3 0.0 copy-start.5
  48.3 0.0 copy-start.6
  48.3 0.0 all-reduce.2.cloned.1.call-update
  48.3 0.0 copy-start.2
  48.3 0.0 copy-start.3
  48.4 0.6 copy-done.1
  49.0 0.0 copy-done.5
  49.0 0.0 copy-done.6
  49.0 0.2 select_reduce_fusion.3
  49.2 0.1 select_reduce_fusion
  49.3 34.9 %psum.15 = s32[2048]{0:T(1024)S(1)} all-reduce(s32[2048]{0:T(1024)S(1)} %and_convert_fusion), channel_id=1, replica_groups=mesh['feat'=128,'rows'=4] {'feat'}, use_global_device_ids=true, to_apply=%region_6.7 | all-reduce | flops 2048 | bytes 16384 | tf_op jit(solution)/shard_map/psum | solution.py:45
  84.1 0.1 fusion.12
  84.2 0.6 multiply_add_fusion
  84.8 0.1 fusion.10
  84.9 33.3 %all-reduce.2.cloned.1.call-done = bf16[32,2,64,256]{3,2,1,0:T(8,128)(2,1)} async-done(((bf16[32,2,64,256]{3,2,1,0:T(8,128)(2,1)}), bf16[32,2,64,256]{3,2,1,0:T(8,128)(2,1)}) %all-reduce.2.cloned.1.call-update) | async-done | bytes 2097168 | tf_op jit(solution)/shard_map/psum | solution.py:64
  118.2 2.0 fusion.8
  120.2 0.1 fusion.7
  120.3 377.4 %all-gather.1 = f32[128,32,4]{1,2,0:T(4,128)S(1)} all-gather(f32[1,32,4]{1,2,0:T(4,128)S(1)} %maximum_bitcast_fusion), channel_id=2, replica_groups=mesh['feat'=128,'rows'=4] {'feat'}, dimensions={0}, use_global_device_ids=true | all-gather | bytes 66048 | tf_op jit(solution)/shard_map/all_gather | solution.py:67
  497.7 0.1 reduce_sum.77
  497.9 0.2 select_reduce_fusion.1
  498.0 0.0 copy-done.2
  498.0 0.0 copy-done.3
  498.1 0.0 copy-start.4
  498.1 0.6 pad_maximum_fusion.1
  498.7 2.1 dynamic-slice_convert_fusion
  500.8 0.0 copy-done.4
  (15 shorter events, 0.2 us)
Async XLA Ops:
  7.2 2.9 copy-start
  7.2 111.0 %all-reduce.2.cloned.1.call-start = ((), (), s32[]{:S(2)}) async-start(), calls=%async_computation | async-start | bytes 4194304 | tf_op jit(solution)/shard_map/psum | solution.py:64
  48.3 0.7 copy-start.1
  48.3 0.7 copy-start.5
  48.3 0.7 copy-start.6
  48.3 449.7 %copy-start.2 = (f32[2048]{0:T(1024)S(1)}, f32[2048]{0:T(1024)}, u32[]{:S(2)}) copy-start(f32[2048]{0:T(1024)} %param.11) | copy-start | bytes 24580
  48.3 449.7 %copy-start.3 = (f32[2048]{0:T(1024)S(1)}, f32[2048]{0:T(1024)}, u32[]{:S(2)}) copy-start(f32[2048]{0:T(1024)} %param.10) | copy-start | bytes 24580
  498.1 2.8 copy-start.4
Sparse Core Ops, SparseCore 0:
  48.4 69.6 all-reduce.1
